TPU v7x, 32 devices: a whole 2x2x4 slice. The times are simulated.
32 devices in a mesh: replica: 16 (over z, x, core), shard: 2 (over y).
Axes of the slice: x: 2, y: 2, z: 4, core: 2. Of those that a mesh axis runs over, the one named last changes fastest.
Arguments:
- latents: bfloat16 [32, 1024, 1152], P('replica', 'shard'), may hold values from -6 to 6
- conditions: bfloat16 [32, 1152], P('replica'), may hold values from -6 to 6
- cotangent: bfloat16 [32, 1024, 1152], P('replica', 'shard'), may hold values from -6 to 6
- counts: int32 [16], P('replica'), may hold values from 1 to 2, as said below
- w_ada: bfloat16 [1152, 6912], P('shard'), may hold values from -0.1875 to 0.1875
- b_ada: bfloat16 [6912], P('shard'), may hold values from -3 to 3
- w_qkv: bfloat16 [1152, 3456], P('shard'), may hold values from -0.1875 to 0.1875
- b_qv: bfloat16 [2304], P('shard'), may hold values from -3 to 3
- w_proj: bfloat16 [1152, 1152], P('shard'), may hold values from -3.5 to 3.5
- b_proj: bfloat16 [1152], P('shard'), may hold values from -3 to 3
- w_fc1: bfloat16 [1152, 4608], P('shard'), may hold values from -0.1875 to 0.1875
- b_fc1: bfloat16 [4608], P('shard'), may hold values from -3 to 3
- w_fc2: bfloat16 [4608, 1152], P('shard'), may hold values from -0.09375 to 0.09375
- b_fc2: bfloat16 [1152], P('shard'), may hold values from -3 to 3
Outputs:
- output: bfloat16 [32, 1024, 1152], P('replica', 'shard')
- grad_latents: float32 [32, 1024, 1152], P('replica', 'shard')
- grad_conditions: float32 [32, 1152], P('replica')
- grad_w_ada: float32 [1152, 6912], P('shard')
- grad_b_ada: float32 [6912], P('shard')
- grad_w_qkv: float32 [1152, 3456], P('shard')
- grad_b_qv: float32 [2304], P('shard')
- grad_w_proj: float32 [1152, 1152], P('shard')
- grad_b_proj: float32 [1152], P('shard')
- grad_w_fc1: float32 [1152, 4608], P('shard')
- grad_b_fc1: float32 [4608], P('shard')
- grad_w_fc2: float32 [4608, 1152], P('shard')
- grad_b_fc2: float32 [1152], P('shard')
Inputs may be any that keep to these rules, and one draw needn't show every extreme that they name: counts[r] live slots on replica r are its slots 0 to counts[r] - 1 of 2; some replica has all 2 live.
All inputs are finite; a program needn't handle non-finite values.
Results may differ from a plain program's by a relative error of at most 0.019.
Values may be sent and summed in bfloat16 or wider, within the bound.
A program may use at most 512 MiB of HBM per device.

v0:
```python
from functools import partial
import math
import jax
import jax.numpy as jnp
from jax import lax
from jax.sharding import PartitionSpec as P

HEADS = 16
HDIM = 72
epsilon = 1e-06


def layer_stats(values):
    centered = values - jnp.mean(values, axis=-1, keepdims=True)
    inverse = lax.rsqrt(jnp.mean(centered * centered, axis=-1, keepdims=True) + epsilon)
    return (centered * inverse, inverse)


def layer_back(normal, inverse, d_normal):
    first_mean = jnp.mean(d_normal, axis=-1, keepdims=True)
    second_mean = jnp.mean(d_normal * normal, axis=-1, keepdims=True)
    return inverse * (d_normal - first_mean - normal * second_mean)


def contract_last(left, right):
    return lax.dot_general(
        left, right, (((1,), (1,)), ((), ())), preferred_element_type=jnp.float32
    )


def forward_product(inputs, whole_pair):
    return (
        jnp.dot(inputs, whole_pair[0], preferred_element_type=jnp.float32),
        whole_pair[1].astype(jnp.float32),
    )


def backward_product(grads, whole_pair):
    return contract_last(grads, whole_pair[0])


def owner_grads(inputs, grads, weight_rows, bias_terms):
    columns = lax.slice_in_dim(inputs, 0, weight_rows * lax.axis_size("shard"), axis=1)
    weight_grad = lax.psum_scatter(
        lax.dot_general(
            columns, grads, (((0,), (0,)), ((), ())), preferred_element_type=jnp.float32
        ).astype(jnp.bfloat16),
        "shard",
        scatter_dimension=0,
        tiled=True,
    ).astype(jnp.float32)
    bias_grad = lax.psum_scatter(
        bias_terms.astype(jnp.bfloat16), "shard", scatter_dimension=0, tiled=True
    ).astype(jnp.float32)
    return (weight_grad, bias_grad)


def shards(
    latents,
    conditions,
    cotangent,
    counts,
    w_ada,
    b_ada,
    w_qkv,
    b_qv,
    w_proj,
    b_proj,
    w_fc1,
    b_fc1,
    w_fc2,
    b_fc2,
):
    slots, block, width = latents.shape
    n_rows = slots * block
    scale = 1.0 / math.sqrt(HDIM)
    live = (jnp.arange(slots, dtype=jnp.int32) < counts[0]).astype(jnp.float32)[:, None, None]
    gathered = (
        lax.all_gather(w_ada, "shard", axis=0, tiled=True),
        lax.all_gather(b_ada, "shard", axis=0, tiled=True),
        lax.all_gather(w_qkv, "shard", axis=0, tiled=True),
        lax.all_gather(b_qv, "shard", axis=0, tiled=True),
        lax.all_gather(w_proj, "shard", axis=0, tiled=True),
        lax.all_gather(b_proj, "shard", axis=0, tiled=True),
        lax.all_gather(w_fc1, "shard", axis=0, tiled=True),
        lax.all_gather(b_fc1, "shard", axis=0, tiled=True),
        lax.all_gather(w_fc2, "shard", axis=0, tiled=True),
        lax.all_gather(b_fc2, "shard", axis=0, tiled=True),
    )
    full_ada = (gathered[0], gathered[1])
    full_qkv = (gathered[2], gathered[3])
    full_proj = (gathered[4], gathered[5])
    full_fc1 = (gathered[6], gathered[7])
    full_fc2 = (gathered[8], gathered[9])
    cond_float = conditions.astype(jnp.float32)
    cond_act = jax.nn.silu(cond_float).astype(jnp.bfloat16)
    ada_prod, ada_bias = forward_product(cond_act, full_ada)
    modul = ada_prod + ada_bias
    shift_a, scale_a, gate_a, shift_m, scale_m, gate_m = [
        piece[:, None, :] for piece in jnp.split(modul, 6, axis=1)
    ]
    tokens = latents.astype(jnp.float32)
    norm_a, inv_a = layer_stats(tokens)
    normed = (norm_a * (1.0 + scale_a) + shift_a).astype(jnp.bfloat16).reshape(n_rows, width)
    qkv_prod, qv_bias = forward_product(normed, full_qkv)
    query = (
        (qkv_prod[:, :width] + qv_bias[:width])
        .astype(jnp.bfloat16)
        .reshape(slots, block, HEADS, HDIM)
    )
    keys_own = qkv_prod[:, width : 2 * width].astype(jnp.bfloat16).reshape(slots, block, width)
    values_own = (
        (qkv_prod[:, 2 * width :] + qv_bias[width:])
        .astype(jnp.bfloat16)
        .reshape(slots, block, width)
    )
    keys_all, values_all = (
        lax.all_gather(keys_own, "shard", axis=1, tiled=True),
        lax.all_gather(values_own, "shard", axis=1, tiled=True),
    )
    length = keys_all.shape[1]
    keys_h = keys_all.reshape(slots, length, HEADS, HDIM)
    values_h = values_all.reshape(slots, length, HEADS, HDIM)
    scores = (
        jnp.einsum("sqhd,skhd->shqk", query, keys_h, preferred_element_type=jnp.float32) * scale
    )
    top_score = jnp.max(scores, axis=-1, keepdims=True)
    log_total = top_score + jnp.log(jnp.sum(jnp.exp(scores - top_score), axis=-1, keepdims=True))
    probs_low = jnp.exp(scores - log_total).astype(jnp.bfloat16)
    attended = jnp.einsum(
        "shqk,skhd->sqhd", probs_low, values_h, preferred_element_type=jnp.float32
    )
    attended = attended.astype(jnp.bfloat16).reshape(n_rows, width)
    proj_prod, proj_bias = forward_product(attended, full_proj)
    branch_a = (proj_prod + proj_bias).reshape(slots, block, width)
    resid = tokens + gate_a * branch_a
    norm_m, inv_m = layer_stats(resid)
    mixed = (norm_m * (1.0 + scale_m) + shift_m).astype(jnp.bfloat16).reshape(n_rows, width)
    fc1_prod, fc1_bias = forward_product(mixed, full_fc1)
    activated, gelu_back = jax.vjp(partial(jax.nn.gelu, approximate=True), fc1_prod + fc1_bias)
    hidden = activated.astype(jnp.bfloat16)
    fc2_prod, fc2_bias = forward_product(hidden, full_fc2)
    branch_m = (fc2_prod + fc2_bias).reshape(slots, block, width)
    final = resid + gate_m * branch_m
    output = (final * live).astype(jnp.bfloat16)
    d_out = cotangent.astype(jnp.float32) * live
    d_gate_m = jnp.sum(d_out * branch_m, axis=1)
    d_branch_m = (gate_m * d_out).astype(jnp.bfloat16).reshape(n_rows, width)
    pair_fc2 = owner_grads(
        hidden, d_branch_m, w_fc2.shape[0], jnp.sum(d_branch_m, axis=0, dtype=jnp.float32)
    )
    d_hidden = backward_product(d_branch_m, full_fc2)
    d_pre = gelu_back(d_hidden)[0].astype(jnp.bfloat16)
    pair_fc1 = owner_grads(mixed, d_pre, w_fc1.shape[0], jnp.sum(d_pre, axis=0, dtype=jnp.float32))
    d_mixed = backward_product(d_pre, full_fc1).reshape(slots, block, width)
    d_shift_m = jnp.sum(d_mixed, axis=1)
    d_scale_m = jnp.sum(d_mixed * norm_m, axis=1)
    d_resid = d_out + layer_back(norm_m, inv_m, d_mixed * (1.0 + scale_m))
    d_gate_a = jnp.sum(d_resid * branch_a, axis=1)
    d_branch_a = (gate_a * d_resid).astype(jnp.bfloat16).reshape(n_rows, width)
    pair_proj = owner_grads(
        attended, d_branch_a, w_proj.shape[0], jnp.sum(d_branch_a, axis=0, dtype=jnp.float32)
    )
    d_attended = (
        backward_product(d_branch_a, full_proj)
        .astype(jnp.bfloat16)
        .reshape(slots, block, HEADS, HDIM)
    )
    scores = (
        jnp.einsum("sqhd,skhd->shqk", query, keys_h, preferred_element_type=jnp.float32) * scale
    )
    probs = jnp.exp(scores - log_total)
    d_probs = jnp.einsum(
        "sqhd,skhd->shqk", d_attended, values_h, preferred_element_type=jnp.float32
    )
    inner = jnp.sum(d_probs * probs, axis=-1, keepdims=True)
    d_scores = (probs * (d_probs - inner)).astype(jnp.bfloat16)
    d_query = (
        (
            jnp.einsum("shqk,skhd->sqhd", d_scores, keys_h, preferred_element_type=jnp.float32)
            * scale
        )
        .astype(jnp.bfloat16)
        .reshape(n_rows, width)
    )
    key_terms = (
        jnp.einsum("shqk,sqhd->skhd", d_scores, query, preferred_element_type=jnp.float32).reshape(
            slots, length, width
        )
        * scale
    )
    value_terms = jnp.einsum(
        "shqk,sqhd->skhd",
        probs.astype(jnp.bfloat16),
        d_attended,
        preferred_element_type=jnp.float32,
    ).reshape(slots, length, width)
    d_keys, d_values = (
        lax.psum_scatter(
            key_terms.astype(jnp.bfloat16), "shard", scatter_dimension=1, tiled=True
        ).astype(jnp.float32),
        lax.psum_scatter(
            value_terms.astype(jnp.bfloat16), "shard", scatter_dimension=1, tiled=True
        ).astype(jnp.float32),
    )
    d_keys = d_keys.astype(jnp.bfloat16).reshape(n_rows, width)
    d_values = d_values.astype(jnp.bfloat16).reshape(n_rows, width)
    d_qkv = jnp.concatenate([d_query, d_keys, d_values], axis=1)
    qv_terms = jnp.concatenate(
        [jnp.sum(d_query, axis=0, dtype=jnp.float32), jnp.sum(d_values, axis=0, dtype=jnp.float32)]
    )
    pair_qkv = owner_grads(normed, d_qkv, w_qkv.shape[0], qv_terms)
    d_normed = backward_product(d_qkv, full_qkv).reshape(slots, block, width)
    d_shift_a = jnp.sum(d_normed, axis=1)
    d_scale_a = jnp.sum(d_normed * norm_a, axis=1)
    grad_latents = d_resid + layer_back(norm_a, inv_a, d_normed * (1.0 + scale_a))
    d_modul_part = jnp.concatenate(
        [d_shift_a, d_scale_a, d_gate_a, d_shift_m, d_scale_m, d_gate_m], axis=1
    )
    d_modul = lax.psum(d_modul_part.astype(jnp.bfloat16), "shard")
    index = lax.axis_index("shard")
    ada_rows = w_ada.shape[0]
    ada_length = b_ada.shape[0]
    own_cond = lax.dynamic_slice_in_dim(cond_act, index * ada_rows, ada_rows, 1)
    grad_w_ada = lax.dot_general(
        own_cond, d_modul, (((0,), (0,)), ((), ())), preferred_element_type=jnp.float32
    )
    grad_b_ada = lax.dynamic_slice_in_dim(
        jnp.sum(d_modul, axis=0, dtype=jnp.float32), index * ada_length, ada_length, 0
    )
    pair_ada = (grad_w_ada, grad_b_ada)
    d_cond_act = backward_product(d_modul, full_ada)
    _, silu_back = jax.vjp(jax.nn.silu, cond_float)
    grad_conditions = silu_back(d_cond_act)[0]
    summed = (
        lax.psum(pair_ada[0].astype(jnp.bfloat16), "replica").astype(jnp.float32),
        lax.psum(pair_ada[1].astype(jnp.bfloat16), "replica").astype(jnp.float32),
        lax.psum(pair_qkv[0].astype(jnp.bfloat16), "replica").astype(jnp.float32),
        lax.psum(pair_qkv[1].astype(jnp.bfloat16), "replica").astype(jnp.float32),
        lax.psum(pair_proj[0].astype(jnp.bfloat16), "replica").astype(jnp.float32),
        lax.psum(pair_proj[1].astype(jnp.bfloat16), "replica").astype(jnp.float32),
        lax.psum(pair_fc1[0].astype(jnp.bfloat16), "replica").astype(jnp.float32),
        lax.psum(pair_fc1[1].astype(jnp.bfloat16), "replica").astype(jnp.float32),
        lax.psum(pair_fc2[0].astype(jnp.bfloat16), "replica").astype(jnp.float32),
        lax.psum(pair_fc2[1].astype(jnp.bfloat16), "replica").astype(jnp.float32),
    )
    pair_ada = (summed[0], summed[1])
    pair_qkv = (summed[2], summed[3])
    pair_proj = (summed[4], summed[5])
    pair_fc1 = (summed[6], summed[7])
    pair_fc2 = (summed[8], summed[9])
    return (
        output,
        grad_latents,
        grad_conditions,
        pair_ada[0],
        pair_ada[1],
        pair_qkv[0],
        pair_qkv[1],
        pair_proj[0],
        pair_proj[1],
        pair_fc1[0],
        pair_fc1[1],
        pair_fc2[0],
        pair_fc2[1],
    )


def solution(mesh):
    placed = (
        P("replica", "shard", None),
        P("replica", None),
        P("replica", "shard", None),
        P("replica"),
        P("shard", None),
        P("shard"),
        P("shard", None),
        P("shard"),
        P("shard", None),
        P("shard"),
        P("shard", None),
        P("shard"),
        P("shard", None),
        P("shard"),
    )
    return jax.shard_map(
        shards,
        mesh=mesh,
        in_specs=placed,
        out_specs=(
            P("replica", "shard", None),
            P("replica", "shard", None),
            P("replica", None),
            P("shard", None),
            P("shard"),
            P("shard", None),
            P("shard"),
            P("shard", None),
            P("shard"),
            P("shard", None),
            P("shard"),
            P("shard", None),
            P("shard"),
        ),
        check_vma=False,
    )
```

profile of v0, /device:TPU:0, one launch (start us, length us, event | category | flops | bytes accessed | tf_op | source)
XLA Modules:
  0.0 1932.2 jit_solution(709824558595214177)
XLA Ops:
  15.4 186.2 %all-gather.11.cloned.1.call-done = bf16[1152,6912]{1,0:T(8,128)(2,1)} async-done(((bf16[576,6912]{1,0:T(8,128)(2,1)}), bf16[1152,6912]{1,0:T(8,128)(2,1)}) %all-gather.11.cloned.1.call-update) | async-done | bytes 15925264 | tf_op jit(solution)/shard_map/all_gather | solution.py:79
  211.7 90.6 %all-gather.13.cloned.1.call-done = bf16[1152,3456]{1,0:T(8,128)(2,1)} async-done(((bf16[576,3456]{1,0:T(8,128)(2,1)}), bf16[1152,3456]{1,0:T(8,128)(2,1)}) %all-gather.13.cloned.1.call-update) | async-done | bytes 7962640 | tf_op jit(solution)/shard_map/all_gather | solution.py:81
  392.2 27.5 %multiply_reduce_fusion.1 = (f32[2,16,512]{2,1,0:T(8,128)S(1)}, f32[2,16,512,1024]{3,2,1,0:T(8,128)}) fusion(bf16[2,512,16,72]{1,3,2,0:T(8,128)(2,1)} %copy.64, bf16[2,1024,16,72]{1,3,2,0:T(8,128)(2,1)} %bitcast.98), kind=kOutput, calls=%fused_computation.4 | convolution fusion | flops 2449457152 | bytes 74252288 | tf_op jit(solution)/shard_map/sqhd,skhd->shqk/dot_general | solution.py:125
  419.6 21.3 %exponential_reduce_fusion = f32[2,16,512]{2,1,0:T(8,128)S(1)} fusion(f32[2,16,512,1024]{3,2,1,0:T(8,128)} %get-tuple-element.64, f32[2,16,512]{2,1,0:T(8,128)S(1)} %get-tuple-element.63), kind=kLoop, calls=%fused_computation.3 | loop fusion | flops 50315264 | bytes 67239936 | tf_op jit(solution)/shard_map/reduce_sum | solution.py:128
  456.9 27.9 %convert_bitcast_fusion = bf16[2,512,16,72]{1,3,2,0:T(8,128)(2,1)} fusion(bf16[2,1024,16,72]{1,3,2,0:T(8,128)(2,1)} %bitcast.94, f32[2,16,512,1024]{3,2,1,0:T(8,128)} %get-tuple-element.64, f32[2,16,512]{2,1,0:T(8,128)S(1)} %log_add_fusion), kind=kOutput, calls=%fused_computation.74 | convolution fusion | flops 2467430400 | bytes 74252288 | tf_op jit(solution)/shard_map/shqk,skhd->sqhd/dot_general | solution.py:130
  503.3 120.2 %all-gather.21.cloned.1.call-done = bf16[1152,4608]{1,0:T(8,128)(2,1)} async-done(((bf16[576,4608]{1,0:T(8,128)(2,1)}), bf16[1152,4608]{1,0:T(8,128)(2,1)}) %all-gather.21.cloned.1.call-update) | async-done | bytes 10616848 | tf_op jit(solution)/shard_map/all_gather | solution.py:85
  623.4 19.1 fusion.60
  642.5 113.4 %all-gather.23.cloned.1.call-done = bf16[4608,1152]{1,0:T(8,128)(2,1)} async-done(((bf16[2304,1152]{1,0:T(8,128)(2,1)}), bf16[4608,1152]{1,0:T(8,128)(2,1)}) %all-gather.23.cloned.1.call-update) | async-done | bytes 10616848 | tf_op jit(solution)/shard_map/all_gather | solution.py:87
  756.0 30.4 %fusion.52 = (bf16[4608]{0:T(1024)(128)(2,1)}, bf16[1024,4608]{1,0:T(8,128)(2,1)}) fusion(f32[1024,4608]{1,0:T(8,128)} %fusion.60, f32[4608]{0:T(1024)S(1)} %reshape.203, bf16[1024,1152]{1,0:T(8,128)(2,1)} %bitcast.118, bf16[4608,1152]{1,0:T(8,128)(2,1)} %all-gather.23.cloned.1.call-done), kind=kOutput, calls=%fused_computation.117 | convolution fusion | flops 10975440896 | bytes 41315328 | tf_op jit(solution)/shard_map/dot_general | solution.py:26
  786.3 19.9 %fusion.29 = (f32[1024]{0:T(1024)S(1)}, f32[1024,1152]{1,0:T(8,128)}) fusion(f32[2,1152]{1,0:T(2,128)S(1)} %get-tuple-element.54, bf16[1024,4608]{1,0:T(8,128)(2,1)} %get-tuple-element.41, bf16[1152,4608]{1,0:T(8,128)(2,1)} %all-gather.21.cloned.1.call-done), kind=kOutput, calls=%fused_computation.53 | convolution fusion | flops 10873994240 | bytes 24785920 | tf_op jit(solution)/shard_map/dot_general | solution.py:26
  806.3 20.9 %convolution_add_fusion.1 = f32[1024,1152]{1,0:T(8,128)S(1)} fusion(bf16[4608,1152]{1,0:T(8,128)(2,1)} %all-gather.23.cloned.1.call-done, f32[1152]{0:T(1024)S(1)} %copy-done.40, f32[1024,4608]{1,0:T(8,128)} %fusion.60, f32[4608]{0:T(1024)S(1)} %reshape.203), kind=kOutput, calls=%fused_computation.35 | convolution fusion | flops 10920001536 | bytes 34232832 | tf_op jit(solution)/shard_map/dot_general | solution.py:33
  856.2 26.0 %fusion.32 = bf16[2,16,72,1024]{3,2,1,0:T(8,128)(2,1)} fusion(bf16[2,512,16,72]{1,3,2,0:T(8,128)(2,1)S(1)} %copy.67, f32[2,16,512,1024]{3,2,1,0:T(8,128)} %get-tuple-element.64, f32[2,16,512]{2,1,0:T(8,128)S(1)} %copy-done.10), kind=kOutput, calls=%fused_computation.72 | convolution fusion | flops 2468610048 | bytes 74252288 | tf_op jit(solution)/shard_map/shqk,sqhd->skhd/dot_general | solution.py:192
  889.0 49.1 %multiply_reduce_fusion = (f32[2,16,512]{2,1,0:T(8,128)S(1)}, f32[2,16,512,1024]{3,2,1,0:T(8,128)}) fusion(f32[2,16,512,1024]{3,2,1,0:T(8,128)} %get-tuple-element.64, f32[2,16,512]{2,1,0:T(8,128)S(1)} %copy-done.10, bf16[2,512,16,72]{1,3,2,0:T(8,128)(2,1)S(1)} %copy.67, bf16[2,1024,16,72]{1,3,2,0:T(8,128)(2,1)} %bitcast.95), kind=kOutput, calls=%fused_computation.1 | convolution fusion | flops 2483011584 | bytes 141426688 | tf_op jit(solution)/shard_map/sqhd,skhd->shqk/dot_general | solution.py:173
  938.2 53.3 %multiply_convert_fusion = bf16[2,16,512,1024]{3,2,1,0:T(8,128)(2,1)} fusion(f32[2,16,512,1024]{3,2,1,0:T(8,128)} %get-tuple-element.68, f32[2,16,512,1024]{3,2,1,0:T(8,128)} %get-tuple-element.64, f32[2,16,512]{2,1,0:T(8,128)S(1)} %get-tuple-element.67, f32[2,16,512]{2,1,0:T(8,128)S(1)} %copy-done.10), kind=kLoop, calls=%fused_computation | loop fusion | flops 83886080 | bytes 167903232 | tf_op jit(solution)/shard_map/convert_element_type | solution.py:177
  991.5 18.7 multiply_convert_fusion.2
  1025.0 23.4 %convolution_convert_fusion = bf16[4608,1152]{1,0:T(8,128)(2,1)} fusion(bf16[1024,1152]{1,0:T(8,128)(2,1)} %bitcast.119, f32[1024,4608]{1,0:T(8,128)} %fusion.60, f32[4608]{0:T(1024)S(1)} %copy-done.33), kind=kOutput, calls=%fused_computation.8 | convolution fusion | flops 10924130304 | bytes 31868928 | tf_op jit(solution)/shard_map/dot_general | solution.py:45
  1050.1 17.4 convolution_convert_fusion.1
  1067.7 18.1 fusion.58
  1113.1 16.0 fusion.28
  1168.5 76.7 %reduce-scatter.17.cloned.1.call-done = bf16[2304,1152]{1,0:T(8,128)(2,1)} async-done(((bf16[4608,1152]{1,0:T(8,128)(2,1)}), bf16[2304,1152]{1,0:T(8,128)(2,1)}) %reduce-scatter.17.cloned.1.call-update) | async-done | bytes 5308432 | tf_op jit(solution)/shard_map/reduce_scatter | solution.py:44
  1245.2 126.1 %reduce-scatter.15.cloned.1.call-done = bf16[576,4608]{1,0:T(8,128)(2,1)} async-done(((bf16[1152,4608]{1,0:T(8,128)(2,1)}), bf16[576,4608]{1,0:T(8,128)(2,1)}) %reduce-scatter.15.cloned.1.call-update) | async-done | bytes 5308432 | tf_op jit(solution)/shard_map/reduce_scatter | solution.py:44
  1371.4 97.6 %reduce-scatter.11.cloned.1.call-done = bf16[576,3456]{1,0:T(8,128)(2,1)} async-done(((bf16[1152,3456]{1,0:T(8,128)(2,1)}), bf16[576,3456]{1,0:T(8,128)(2,1)}) %reduce-scatter.11.cloned.1.call-update) | async-done | bytes 3981328 | tf_op jit(solution)/shard_map/reduce_scatter | solution.py:44
  1471.5 64.6 %all-reduce.6 = (bf16[3456]{0:T(1024)(128)(2,1)S(1)}, bf16[1152]{0:T(1024)(128)(2,1)S(1)}, bf16[576]{0:T(1024)(128)(2,1)S(1)}, bf16[2304]{0:T(1024)(128)(2,1)S(1)}, bf16[576]{0:T(1024)(128)(2,1)S(1)}) all-reduce(bf16[3456]{0:T(1024)(128)(2,1)S(1)} %dynamic_slice.11, ...), channel_id=1, replica_groups=mesh['replica'=16,'shard'=2] {'replica'}, use_global_device_ids=true, to_apply=%region_22.23 | all-reduce | flops 8064 | bytes 32256 | tf_op jit(solution)/shard_map/psum | solution.py:237
  1539.1 356.0 %all-reduce.12.cloned.1.call-done = (bf16[576,6912]{1,0:T(8,128)(2,1)}, bf16[576,3456]{1,0:T(8,128)(2,1)}, bf16[576,1152]{1,0:T(8,128)(2,1)}, bf16[576,4608]{1,0:T(8,128)(2,1)}, bf16[2304,1152]{1,0:T(8,128)(2,1)}) async-done(((bf16[576,6912]{1,0:T(8,128)(2,1)}, bf16[576,3456]{1,0:T(8,128)(2,1)}, bf16[576,1152]{1,0:T(8,128)(2,1)}, bf16[576,4608]{1,0:T(8,128)(2,1)}, bf16[2304,1152]{1,0:T(8,128)(2,1)}), ...) | async-done | bytes 23887888 | tf_op jit(solution)/shard_map/psum | solution.py:236
  (243 shorter events, 293.1 us)
Async XLA Ops:
  7.2 194.4 %all-gather.11.cloned.1.call-start = ((), (), s32[]{:S(2)}) async-start(), calls=%async_computation.6 | async-start | bytes 23887872 | tf_op jit(solution)/shard_map/all_gather | solution.py:79
  7.9 193.7 %copy-start.30 = (bf16[2,1152]{1,0:T(2,128)(2,1)S(1)}, bf16[2,1152]{1,0:T(2,128)(2,1)}, u32[]{:S(2)}) copy-start(bf16[2,1152]{1,0:T(2,128)(2,1)} %param.15) | copy-start | bytes 13828
  7.9 294.4 %all-gather.13.cloned.1.call-start = ((), (), s32[]{:S(2)}) async-start(), calls=%async_computation.7 | async-start | bytes 11943936 | tf_op jit(solution)/shard_map/all_gather | solution.py:81
  8.7 376.9 %all-gather.17.cloned.1.call-start = ((), (), s32[]{:S(2)}) async-start(), calls=%async_computation.9 | async-start | bytes 7077888 | tf_op jit(solution)/shard_map/all_gather | solution.py:118
  14.6 194.7 %copy-start.20 = (f32[2,512]{1,0:T(2,128)}, f32[2,512]{1,0:T(2,128)S(1)}, u32[]{:S(2)}) copy-start(f32[2,512]{1,0:T(2,128)S(1)} %broadcast_multiply_fusion.5) | copy-start | bytes 12292
  15.4 193.9 %copy-start.28 = (f32[2,512]{1,0:T(2,128)}, f32[2,512]{1,0:T(2,128)S(1)}, u32[]{:S(2)}) copy-start(f32[2,512]{1,0:T(2,128)S(1)} %add_rsqrt_fusion.1) | copy-start | bytes 12292
  209.3 106.1 %copy-start.16 = (f32[2,1152]{1,0:T(2,128)}, f32[2,1152]{1,0:T(2,128)S(1)}, u32[]{:S(2)}) copy-start(f32[2,1152]{1,0:T(2,128)S(1)} %get-tuple-element.56) | copy-start | bytes 27652
  209.3 157.2 %copy-start.24 = (f32[2,1152]{1,0:T(2,128)}, f32[2,1152]{1,0:T(2,128)S(1)}, u32[]{:S(2)}) copy-start(f32[2,1152]{1,0:T(2,128)S(1)} %get-tuple-element.52) | copy-start | bytes 27652
  209.3 287.8 %copy-start.22 = (f32[2,1152]{1,0:T(2,128)}, f32[2,1152]{1,0:T(2,128)S(1)}, u32[]{:S(2)}) copy-start(f32[2,1152]{1,0:T(2,128)S(1)} %get-tuple-element.57) | copy-start | bytes 27652
  322.4 127.8 %all-gather.15.cloned.1.call-start = ((), (), s32[]{:S(2)}) async-start(), calls=%async_computation.8 | async-start | bytes 7077888 | tf_op jit(solution)/shard_map/all_gather | solution.py:119
  334.7 156.4 %all-gather.19.cloned.1.call-start = ((), (), s32[]{:S(2)}) async-start(), calls=%async_computation.10 | async-start | bytes 3981312 | tf_op jit(solution)/shard_map/all_gather | solution.py:83
  335.3 288.1 %all-gather.21.cloned.1.call-start = ((), (), s32[]{:S(2)}) async-start(), calls=%async_computation.11 | async-start | bytes 15925248 | tf_op jit(solution)/shard_map/all_gather | solution.py:85
  335.9 420.1 %all-gather.23.cloned.1.call-start = ((), (), s32[]{:S(2)}) async-start(), calls=%async_computation.12 | async-start | bytes 15925248 | tf_op jit(solution)/shard_map/all_gather | solution.py:87
  336.6 753.6 %reduce-scatter.9.cloned.1.call-start = ((), (), s32[]{:S(2)}) async-start(), calls=%async_computation.14 | async-start | bytes 7077888 | tf_op jit(solution)/shard_map/reduce_scatter | solution.py:202
  349.8 456.5 %copy-start.32 = (f32[4608]{0:T(1024)}, f32[4608]{0:T(1024)S(1)}, u32[]{:S(2)}) copy-start(f32[4608]{0:T(1024)S(1)} %reshape.203) | copy-start | bytes 55300
  500.2 142.3 %copy-start.26 = (f32[2,512]{1,0:T(2,128)}, f32[2,512]{1,0:T(2,128)S(1)}, u32[]{:S(2)}) copy-start(f32[2,512]{1,0:T(2,128)S(1)} %add_rsqrt_fusion) | copy-start | bytes 12292
  503.3 139.3 %copy-start.13 = (bf16[2,512,1152]{2,1,0:T(8,128)(2,1)}, bf16[2,512,1152]{2,1,0:T(8,128)(2,1)S(1)}, u32[]{:S(2)}) copy-start(bf16[2,512,1152]{2,1,0:T(8,128)(2,1)S(1)} %add_convert_fusion) | copy-start | bytes 7077892
  889.0 205.6 %reduce-scatter.7.cloned.1.call-start = ((), (), s32[]{:S(2)}) async-start(), calls=%async_computation.13 | async-start | bytes 7077888 | tf_op jit(solution)/shard_map/reduce_scatter | solution.py:199
  938.2 53.3 %copy-start.5 = (bf16[2,512,16,72]{1,3,2,0:T(8,128)(2,1)S(1)}, bf16[2,512,16,72]{1,3,2,0:T(8,128)(2,1)}, u32[]{:S(2)}) copy-start(bf16[2,512,16,72]{1,3,2,0:T(8,128)(2,1)} %copy.64) | copy-start | bytes 7077892
  1016.9 151.6 %reduce-scatter.13.cloned.1.call-start = ((), (), s32[]{:S(2)}) async-start(), calls=%async_computation.16 | async-start | bytes 3981312 | tf_op jit(solution)/shard_map/reduce_scatter | solution.py:44
  1025.0 220.2 %reduce-scatter.17.cloned.1.call-start = ((), (), s32[]{:S(2)}) async-start(), calls=%async_computation.18 | async-start | bytes 15925248 | tf_op jit(solution)/shard_map/reduce_scatter | solution.py:44
  1048.5 322.9 %reduce-scatter.15.cloned.1.call-start = ((), (), s32[]{:S(2)}) async-start(), calls=%async_computation.17 | async-start | bytes 15925248 | tf_op jit(solution)/shard_map/reduce_scatter | solution.py:44
  1067.6 401.3 %reduce-scatter.11.cloned.1.call-start = ((), (), s32[]{:S(2)}) async-start(), calls=%async_computation.15 | async-start | bytes 11943936 | tf_op jit(solution)/shard_map/reduce_scatter | solution.py:44
  1112.4 782.8 %all-reduce.12.cloned.1.call-start = ((), (), s32[]{:S(2)}) async-start(), calls=%async_computation.19 | async-start | bytes 47775744 | tf_op jit(solution)/shard_map/psum | solution.py:236
  (46 other events, 516.5 us)
Sparse Core Ops, SparseCore 0:
  9.6 191.9 all-gather.10
  203.1 99.1 all-gather.12
  322.5 63.0 all-gather.16
  387.5 62.6 all-gather.14
  451.6 39.3 all-gather.18
  492.4 130.9 all-gather.20
  625.0 130.9 all-gather.22
  889.1 59.9 reduce-scatter.8
  1017.0 60.0 reduce-scatter.6
  1079.8 37.9 reduce-scatter.12
  1120.7 124.4 reduce-scatter.16
  1248.1 123.2 reduce-scatter.14
  1374.2 94.6 reduce-scatter.10
  1475.5 419.5 all-reduce.11
where the time goes:
time: 1940 us; the launch traced here: 1930 us
  waiting for transfers between devices  1190 us (61%)
  matrix products  381 us (20%)
  other arithmetic  150 us (8%)
  local copies, waits for them, and re-layouts  94.9 us (5%)
  blocking collectives  93.2 us (5%)
    psum x1, waiting for transfers between devices, shards(): lax.psum(pair_ada[0].astype(jnp.bfloat16), 'replica').astype(jnp.float32)  356 us
    reduce_scatter x4, waiting for transfers between devices, owner_grads(): lax.psum_scatter(lax.dot_general(columns, grads, (((0,), (0,)), ((), ()))...  300 us
    all_gather x1, waiting for transfers between devices, shards(): lax.all_gather(w_ada, 'shard', axis=0, tiled=True)  186 us
    all_gather x1, waiting for transfers between devices, shards(): lax.all_gather(w_fc1, 'shard', axis=0, tiled=True)  120 us
    all_gather x1, waiting for transfers between devices, shards(): lax.all_gather(w_fc2, 'shard', axis=0, tiled=True)  113 us
    all_gather x1, waiting for transfers between devices, shards(): lax.all_gather(w_qkv, 'shard', axis=0, tiled=True)  90.6 us
    dot_general x5, matrix products, contract_last(): lax.dot_general(left, right, (((1,), (1,)), ((), ())), preferred_element_...  80.5 us
    dot_general x5, matrix products, forward_product(): jnp.dot(inputs, whole_pair[0], preferred_element_type=jnp.float32)  66.9 us
  transfers between devices with their start and end apart: 14, of which 11 were waited for; matrix products, arithmetic and copies ran while one was open for 23% of the time, Pallas kernels for 0%

commit v1 on v0

--- a/solution.py
+++ b/solution.py
@@ -8,6 +8,11 @@
 HEADS = 16
 HDIM = 72
 epsilon = 1e-06
+
+
+def summed_here(x, axis):
+    pieces = lax.all_gather(x, axis)
+    return jnp.sum(pieces, axis=0)
 
 
 def layer_stats(values):
@@ -233,7 +238,7 @@
     _, silu_back = jax.vjp(jax.nn.silu, cond_float)
     grad_conditions = silu_back(d_cond_act)[0]
     summed = (
-        lax.psum(pair_ada[0].astype(jnp.bfloat16), "replica").astype(jnp.float32),
+        summed_here(pair_ada[0].astype(jnp.bfloat16), "replica").astype(jnp.float32),
         lax.psum(pair_ada[1].astype(jnp.bfloat16), "replica").astype(jnp.float32),
         lax.psum(pair_qkv[0].astype(jnp.bfloat16), "replica").astype(jnp.float32),
         lax.psum(pair_qkv[1].astype(jnp.bfloat16), "replica").astype(jnp.float32),

time: 1940 us -> 2440 us (1.26)
  waiting for transfers between devices: 1190 us -> 1650 us
  other arithmetic: 150 us -> 195 us
    all_gather x0 -> x1, waiting for transfers between devices: none -> 591 us  [summed_here(): pieces = lax.all_gather(x, axis)]
    psum x1, waiting for transfers between devices: 356 us -> 168 us  [shards(): lax.psum(pair_qkv[0].astype(jnp.bfloat16), 'replica').astype(jnp.float32)]
    reduce_scatter x4, waiting for transfers between devices: 300 us -> 355 us  [owner_grads(): lax.psum_scatter(lax.dot_general(columns, grads, (((0,), (0,)), ((), ()))...]
    reduce_sum x0 -> x1, other arithmetic: none -> 43.4 us  [summed_here(): return jnp.sum(pieces, axis=0)]
  transfers between devices with their start and end apart: 14 -> 15, of which waited for: 11 -> 13; matrix products, arithmetic and copies ran while one was open for 23% -> 19% of each run, Pallas kernels for 0% -> 0%
where the time goes in v1:
time: 2440 us; the launch traced here: 2430 us
  waiting for transfers between devices  1650 us (68%)
  matrix products  381 us (16%)
  other arithmetic  195 us (8%)
  local copies, waits for them, and re-layouts  94.8 us (4%)
  blocking collectives  91 us (4%)
    all_gather x1, waiting for transfers between devices, summed_here(): pieces = lax.all_gather(x, axis)  591 us
    reduce_scatter x4, waiting for transfers between devices, owner_grads(): lax.psum_scatter(lax.dot_general(columns, grads, (((0,), (0,)), ((), ()))...  355 us
    all_gather x1, waiting for transfers between devices, shards(): lax.all_gather(w_ada, 'shard', axis=0, tiled=True)  186 us
    psum x1, waiting for transfers between devices, shards(): lax.psum(pair_qkv[0].astype(jnp.bfloat16), 'replica').astype(jnp.float32)  168 us
    all_gather x1, waiting for transfers between devices, shards(): lax.all_gather(w_fc1, 'shard', axis=0, tiled=True)  120 us
    all_gather x1, waiting for transfers between devices, shards(): lax.all_gather(w_fc2, 'shard', axis=0, tiled=True)  113 us
    all_gather x1, waiting for transfers between devices, shards(): lax.all_gather(w_qkv, 'shard', axis=0, tiled=True)  90.6 us
    dot_general x5, matrix products, contract_last(): lax.dot_general(left, right, (((1,), (1,)), ((), ())), preferred_element_...  80.8 us
  transfers between devices with their start and end apart: 15, of which 13 were waited for; matrix products, arithmetic and copies ran while one was open for 19% of the time, Pallas kernels for 0%

profile of v1, /device:TPU:0, one launch (start us, length us, event | category | flops | bytes accessed | tf_op | source)
XLA Modules:
  0.0 2432.9 jit_solution(6386350697523545702)
XLA Ops:
  15.4 186.2 %all-gather.13.cloned.1.call-done = bf16[1152,6912]{1,0:T(8,128)(2,1)} async-done(((bf16[576,6912]{1,0:T(8,128)(2,1)}), bf16[1152,6912]{1,0:T(8,128)(2,1)}) %all-gather.13.cloned.1.call-update) | async-done | bytes 15925264 | tf_op jit(solution)/shard_map/all_gather | solution.py:84
  211.8 90.6 %all-gather.15.cloned.1.call-done = bf16[1152,3456]{1,0:T(8,128)(2,1)} async-done(((bf16[576,3456]{1,0:T(8,128)(2,1)}), bf16[1152,3456]{1,0:T(8,128)(2,1)}) %all-gather.15.cloned.1.call-update) | async-done | bytes 7962640 | tf_op jit(solution)/shard_map/all_gather | solution.py:86
  392.2 27.5 %multiply_reduce_fusion.1 = (f32[2,16,512]{2,1,0:T(8,128)S(1)}, f32[2,16,512,1024]{3,2,1,0:T(8,128)}) fusion(bf16[2,512,16,72]{1,3,2,0:T(8,128)(2,1)} %copy.64, bf16[2,1024,16,72]{1,3,2,0:T(8,128)(2,1)} %bitcast.99), kind=kOutput, calls=%fused_computation.4 | convolution fusion | flops 2449457152 | bytes 74252288 | tf_op jit(solution)/shard_map/sqhd,skhd->shqk/dot_general | solution.py:130
  419.6 21.3 exponential_reduce_fusion
  456.9 27.9 %convert_bitcast_fusion = bf16[2,512,16,72]{1,3,2,0:T(8,128)(2,1)} fusion(bf16[2,1024,16,72]{1,3,2,0:T(8,128)(2,1)} %bitcast.95, f32[2,16,512,1024]{3,2,1,0:T(8,128)} %get-tuple-element.63, f32[2,16,512]{2,1,0:T(8,128)S(1)} %log_add_fusion), kind=kOutput, calls=%fused_computation.74 | convolution fusion | flops 2467430400 | bytes 74252288 | tf_op jit(solution)/shard_map/shqk,skhd->sqhd/dot_general | solution.py:135
  503.3 120.2 %all-gather.23.cloned.1.call-done = bf16[1152,4608]{1,0:T(8,128)(2,1)} async-done(((bf16[576,4608]{1,0:T(8,128)(2,1)}), bf16[1152,4608]{1,0:T(8,128)(2,1)}) %all-gather.23.cloned.1.call-update) | async-done | bytes 10616848 | tf_op jit(solution)/shard_map/all_gather | solution.py:90
  623.4 19.1 fusion.60
  642.5 113.4 %all-gather.25.cloned.1.call-done = bf16[4608,1152]{1,0:T(8,128)(2,1)} async-done(((bf16[2304,1152]{1,0:T(8,128)(2,1)}), bf16[4608,1152]{1,0:T(8,128)(2,1)}) %all-gather.25.cloned.1.call-update) | async-done | bytes 10616848 | tf_op jit(solution)/shard_map/all_gather | solution.py:92
  756.0 30.6 %fusion.52 = (bf16[4608]{0:T(1024)(128)(2,1)}, bf16[1024,4608]{1,0:T(8,128)(2,1)}) fusion(f32[1024,4608]{1,0:T(8,128)} %fusion.60, f32[4608]{0:T(1024)S(1)} %reshape.204, bf16[1024,1152]{1,0:T(8,128)(2,1)} %bitcast.119, bf16[4608,1152]{1,0:T(8,128)(2,1)} %all-gather.25.cloned.1.call-done), kind=kOutput, calls=%fused_computation.117 | convolution fusion | flops 10975440896 | bytes 41315328 | tf_op jit(solution)/shard_map/dot_general | solution.py:31
  786.6 19.9 fusion.29
  806.6 20.9 convolution_add_fusion.1
  856.5 26.0 %fusion.32 = bf16[2,16,72,1024]{3,2,1,0:T(8,128)(2,1)} fusion(bf16[2,512,16,72]{1,3,2,0:T(8,128)(2,1)S(1)} %copy.67, f32[2,16,512,1024]{3,2,1,0:T(8,128)} %get-tuple-element.63, f32[2,16,512]{2,1,0:T(8,128)S(1)} %copy-done.10), kind=kOutput, calls=%fused_computation.72 | convolution fusion | flops 2468610048 | bytes 74252288 | tf_op jit(solution)/shard_map/shqk,sqhd->skhd/dot_general | solution.py:197
  889.2 49.1 %multiply_reduce_fusion = (f32[2,16,512]{2,1,0:T(8,128)S(1)}, f32[2,16,512,1024]{3,2,1,0:T(8,128)}) fusion(f32[2,16,512,1024]{3,2,1,0:T(8,128)} %get-tuple-element.63, f32[2,16,512]{2,1,0:T(8,128)S(1)} %copy-done.10, bf16[2,512,16,72]{1,3,2,0:T(8,128)(2,1)S(1)} %copy.67, bf16[2,1024,16,72]{1,3,2,0:T(8,128)(2,1)} %bitcast.96), kind=kOutput, calls=%fused_computation.1 | convolution fusion | flops 2483011584 | bytes 141426688 | tf_op jit(solution)/shard_map/sqhd,skhd->shqk/dot_general | solution.py:178
  938.4 53.4 %multiply_convert_fusion = bf16[2,16,512,1024]{3,2,1,0:T(8,128)(2,1)} fusion(f32[2,16,512,1024]{3,2,1,0:T(8,128)} %get-tuple-element.67, f32[2,16,512,1024]{3,2,1,0:T(8,128)} %get-tuple-element.63, f32[2,16,512]{2,1,0:T(8,128)S(1)} %get-tuple-element.66, f32[2,16,512]{2,1,0:T(8,128)S(1)} %copy-done.10), kind=kLoop, calls=%fused_computation | loop fusion | flops 83886080 | bytes 167903232 | tf_op jit(solution)/shard_map/convert_element_type | solution.py:182
  991.8 18.7 multiply_convert_fusion.2
  1025.3 23.5 convolution_convert_fusion
  1068.0 18.1 fusion.58
  1118.0 126.2 %reduce-scatter.17.cloned.1.call-done = bf16[2304,1152]{1,0:T(8,128)(2,1)} async-done(((bf16[4608,1152]{1,0:T(8,128)(2,1)}), bf16[2304,1152]{1,0:T(8,128)(2,1)}) %reduce-scatter.17.cloned.1.call-update) | async-done | bytes 5308432 | tf_op jit(solution)/shard_map/reduce_scatter | solution.py:49
  1244.2 126.2 %reduce-scatter.15.cloned.1.call-done = bf16[576,4608]{1,0:T(8,128)(2,1)} async-done(((bf16[1152,4608]{1,0:T(8,128)(2,1)}), bf16[576,4608]{1,0:T(8,128)(2,1)}) %reduce-scatter.15.cloned.1.call-update) | async-done | bytes 5308432 | tf_op jit(solution)/shard_map/reduce_scatter | solution.py:49
  1370.4 97.6 %reduce-scatter.11.cloned.1.call-done = bf16[576,3456]{1,0:T(8,128)(2,1)} async-done(((bf16[1152,3456]{1,0:T(8,128)(2,1)}), bf16[576,3456]{1,0:T(8,128)(2,1)}) %reduce-scatter.11.cloned.1.call-update) | async-done | bytes 3981328 | tf_op jit(solution)/shard_map/reduce_scatter | solution.py:49
  1524.8 63.8 %all-reduce.6 = (bf16[3456]{0:T(1024)(128)(2,1)S(1)}, bf16[1152]{0:T(1024)(128)(2,1)S(1)}, bf16[576]{0:T(1024)(128)(2,1)S(1)}, bf16[2304]{0:T(1024)(128)(2,1)S(1)}, bf16[576]{0:T(1024)(128)(2,1)S(1)}) all-reduce(bf16[3456]{0:T(1024)(128)(2,1)S(1)} %dynamic_slice.11, ...), channel_id=1, replica_groups=mesh['replica'=16,'shard'=2] {'replica'}, use_global_device_ids=true, to_apply=%region_22.23 | all-reduce | flops 8064 | bytes 32256 | tf_op jit(solution)/shard_map/psum | solution.py:242
  1591.6 168.3 %all-reduce.12.cloned.1.call-done = (bf16[576,3456]{1,0:T(8,128)(2,1)}, bf16[576,1152]{1,0:T(8,128)(2,1)}, bf16[576,4608]{1,0:T(8,128)(2,1)}, bf16[2304,1152]{1,0:T(8,128)(2,1)}) async-done(((bf16[576,3456]{1,0:T(8,128)(2,1)}, bf16[576,1152]{1,0:T(8,128)(2,1)}, bf16[576,4608]{1,0:T(8,128)(2,1)}, bf16[2304,1152]{1,0:T(8,128)(2,1)}), (bf16[576,3456]{1,0:T(8,128)(2,1)}, bf16[576,1152]{1,0:T(8,128)(2,1)}, ...) | async-done | bytes 15925264 | tf_op jit(solution)/shard_map/psum | solution.py:243
  1781.0 591.2 %all-gather.27.cloned.1.call-done = bf16[9216,6912]{1,0:T(8,128)(2,1)} async-done(((bf16[576,6912]{1,0:T(8,128)(2,1)}), bf16[9216,6912]{1,0:T(8,128)(2,1)}) %all-gather.27.cloned.1.call-update) | async-done | bytes 127402000 | tf_op jit(solution)/shard_map/all_gather | solution.py:14
  2372.2 43.4 %reduce_sum.237 = bf16[576,6912]{1,0:T(8,128)(2,1)} reduce(bf16[16,576,6912]{2,1,0:T(8,128)(2,1)} %bitcast.24, bf16[]{:T(256)} %constant.53.clone.1), dimensions={0}, to_apply=%region_20.21 | reduce | flops 59719680 | bytes 135364608 | tf_op jit(solution)/shard_map/reduce_sum | solution.py:15
  (249 shorter events, 331.6 us)
Async XLA Ops:
  7.2 194.4 %all-gather.13.cloned.1.call-start = ((), (), s32[]{:S(2)}) async-start(), calls=%async_computation.6 | async-start | bytes 23887872 | tf_op jit(solution)/shard_map/all_gather | solution.py:84
  7.9 193.7 %copy-start.31 = (bf16[2,1152]{1,0:T(2,128)(2,1)S(1)}, bf16[2,1152]{1,0:T(2,128)(2,1)}, u32[]{:S(2)}) copy-start(bf16[2,1152]{1,0:T(2,128)(2,1)} %param.15) | copy-start | bytes 13828
  7.9 294.4 %all-gather.15.cloned.1.call-start = ((), (), s32[]{:S(2)}) async-start(), calls=%async_computation.7 | async-start | bytes 11943936 | tf_op jit(solution)/shard_map/all_gather | solution.py:86
  8.7 376.9 %all-gather.19.cloned.1.call-start = ((), (), s32[]{:S(2)}) async-start(), calls=%async_computation.9 | async-start | bytes 7077888 | tf_op jit(solution)/shard_map/all_gather | solution.py:123
  14.6 194.7 %copy-start.21 = (f32[2,512]{1,0:T(2,128)}, f32[2,512]{1,0:T(2,128)S(1)}, u32[]{:S(2)}) copy-start(f32[2,512]{1,0:T(2,128)S(1)} %broadcast_multiply_fusion.5) | copy-start | bytes 12292
  15.4 193.9 %copy-start.29 = (f32[2,512]{1,0:T(2,128)}, f32[2,512]{1,0:T(2,128)S(1)}, u32[]{:S(2)}) copy-start(f32[2,512]{1,0:T(2,128)S(1)} %add_rsqrt_fusion.1) | copy-start | bytes 12292
  209.3 106.1 %copy-start.17 = (f32[2,1152]{1,0:T(2,128)}, f32[2,1152]{1,0:T(2,128)S(1)}, u32[]{:S(2)}) copy-start(f32[2,1152]{1,0:T(2,128)S(1)} %get-tuple-element.55) | copy-start | bytes 27652
  209.3 157.2 %copy-start.25 = (f32[2,1152]{1,0:T(2,128)}, f32[2,1152]{1,0:T(2,128)S(1)}, u32[]{:S(2)}) copy-start(f32[2,1152]{1,0:T(2,128)S(1)} %get-tuple-element.51) | copy-start | bytes 27652
  209.3 287.8 %copy-start.23 = (f32[2,1152]{1,0:T(2,128)}, f32[2,1152]{1,0:T(2,128)S(1)}, u32[]{:S(2)}) copy-start(f32[2,1152]{1,0:T(2,128)S(1)} %get-tuple-element.56) | copy-start | bytes 27652
  322.4 127.8 %all-gather.17.cloned.1.call-start = ((), (), s32[]{:S(2)}) async-start(), calls=%async_computation.8 | async-start | bytes 7077888 | tf_op jit(solution)/shard_map/all_gather | solution.py:124
  334.7 156.4 %all-gather.21.cloned.1.call-start = ((), (), s32[]{:S(2)}) async-start(), calls=%async_computation.10 | async-start | bytes 3981312 | tf_op jit(solution)/shard_map/all_gather | solution.py:88
  335.3 288.1 %all-gather.23.cloned.1.call-start = ((), (), s32[]{:S(2)}) async-start(), calls=%async_computation.11 | async-start | bytes 15925248 | tf_op jit(solution)/shard_map/all_gather | solution.py:90
  335.9 420.1 %all-gather.25.cloned.1.call-start = ((), (), s32[]{:S(2)}) async-start(), calls=%async_computation.12 | async-start | bytes 15925248 | tf_op jit(solution)/shard_map/all_gather | solution.py:92
  336.6 753.9 %reduce-scatter.9.cloned.1.call-start = ((), (), s32[]{:S(2)}) async-start(), calls=%async_computation.14 | async-start | bytes 7077888 | tf_op jit(solution)/shard_map/reduce_scatter | solution.py:207
  349.7 456.7 %copy-start.33 = (f32[4608]{0:T(1024)}, f32[4608]{0:T(1024)S(1)}, u32[]{:S(2)}) copy-start(f32[4608]{0:T(1024)S(1)} %reshape.204) | copy-start | bytes 55300
  500.2 142.3 %copy-start.27 = (f32[2,512]{1,0:T(2,128)}, f32[2,512]{1,0:T(2,128)S(1)}, u32[]{:S(2)}) copy-start(f32[2,512]{1,0:T(2,128)S(1)} %add_rsqrt_fusion) | copy-start | bytes 12292
  503.3 139.3 %copy-start.14 = (bf16[2,512,1152]{2,1,0:T(8,128)(2,1)}, bf16[2,512,1152]{2,1,0:T(8,128)(2,1)S(1)}, u32[]{:S(2)}) copy-start(bf16[2,512,1152]{2,1,0:T(8,128)(2,1)S(1)} %add_convert_fusion) | copy-start | bytes 7077892
  889.2 205.7 %reduce-scatter.7.cloned.1.call-start = ((), (), s32[]{:S(2)}) async-start(), calls=%async_computation.13 | async-start | bytes 7077888 | tf_op jit(solution)/shard_map/reduce_scatter | solution.py:204
  1017.2 100.8 %reduce-scatter.13.cloned.1.call-start = ((), (), s32[]{:S(2)}) async-start(), calls=%async_computation.16 | async-start | bytes 3981312 | tf_op jit(solution)/shard_map/reduce_scatter | solution.py:49
  1025.2 219.0 %reduce-scatter.17.cloned.1.call-start = ((), (), s32[]{:S(2)}) async-start(), calls=%async_computation.18 | async-start | bytes 15925248 | tf_op jit(solution)/shard_map/reduce_scatter | solution.py:49
  1048.8 321.5 %reduce-scatter.15.cloned.1.call-start = ((), (), s32[]{:S(2)}) async-start(), calls=%async_computation.17 | async-start | bytes 15925248 | tf_op jit(solution)/shard_map/reduce_scatter | solution.py:49
  1067.9 400.0 %reduce-scatter.11.cloned.1.call-start = ((), (), s32[]{:S(2)}) async-start(), calls=%async_computation.15 | async-start | bytes 11943936 | tf_op jit(solution)/shard_map/reduce_scatter | solution.py:49
  1112.6 647.2 %all-reduce.12.cloned.1.call-start = ((), (), s32[]{:S(2)}) async-start(), calls=%async_computation.20 | async-start | bytes 31850496 | tf_op jit(solution)/shard_map/psum | solution.py:243
  1468.0 904.2 %all-gather.27.cloned.1.call-start = ((), (), s32[]{:S(2)}) async-start(), calls=%async_computation.19 | async-start | bytes 135364608 | tf_op jit(solution)/shard_map/all_gather | solution.py:14
  (48 other events, 550.5 us)
Sparse Core Ops, SparseCore 0:
  9.6 191.9 all-gather.12
  203.1 99.1 all-gather.14
  322.5 63.0 all-gather.18
  387.5 62.6 all-gather.16
  451.6 39.3 all-gather.20
  492.4 130.9 all-gather.22
  625.0 130.9 all-gather.24
  889.3 59.9 reduce-scatter.8
  1017.3 59.9 reduce-scatter.6
  1080.0 37.9 reduce-scatter.12
  1120.9 123.2 reduce-scatter.16
  1247.0 123.2 reduce-scatter.14
  1373.2 94.6 reduce-scatter.10
  1473.0 286.7 all-reduce.11
  1762.0 610.1 all-gather.26
